TPU v7x, 512 devices: a whole 4x8x8 slice. The times are simulated.
512 devices in a mesh: col: 128 (over z, y, core), row: 4 (over x).
Axes of the slice: x: 4, y: 8, z: 8, core: 2. Of those that a mesh axis runs over, the one named last changes fastest.
Arguments:
- panel: int32 [128], replicated, may hold values from 0 to 127, each once
- centres_cols: bfloat16 [65536, 1024], P('col'), may hold values from -1 to 1
- centres_rows: bfloat16 [2048, 1024], P(('row', 'col')), may hold values from -1 to 1
- diag_inverse: float32 [65536, 512], P('col'), as said below
- trailing: float32 [2048, 65536], P('row', 'col'), may hold values from -6 to 6
Outputs:
- updated: float32 [2048, 65536], P('row', 'col')
Inputs may be any that keep to these rules, and one draw needn't show every extreme that they name: panel holds each of 0 to 127 once. Each 512 x 512 block of diag_inverse is lower triangular with a positive diagonal.
All inputs are finite; a program needn't handle non-finite values.
Results may differ from a plain program's by a relative error of at most 0.0003.
Values may be sent and summed in bfloat16 or wider, within the bound.
No kernel may reach another device: no remote copies, remote signals or barrier semaphores. Data moves between devices by JAX's collectives and lax.ppermute only.
A program may use at most 64 MiB of HBM per device.

v0:
```python
import math
import jax
import jax.numpy as jnp
from jax import lax
from jax.sharding import PartitionSpec as P

LAYERS = 3


def broadcast(shard, axis, root):
    mine = lax.axis_index(axis) == root
    return lax.psum(jnp.where(mine, shard, jnp.zeros_like(shard)), axis)


def kernel(left, right):
    gram = lax.dot_general(
        left, right, (((1,), (1,)), ((), ())), preferred_element_type=jnp.float32
    )
    left_f = left.astype(jnp.float32)
    right_f = right.astype(jnp.float32)
    inv_left = 1.0 / jnp.sqrt(jnp.sum(left_f * left_f, axis=1) + 1e-06)
    inv_right = 1.0 / jnp.sqrt(jnp.sum(right_f * right_f, axis=1) + 1e-06)
    cosine = gram * inv_left[:, None] * inv_right[None, :]
    theta = cosine
    rho_now = cosine
    for layer in range(LAYERS):
        angle_now = jnp.arccos(rho_now)
        zero_order = (math.pi - angle_now) / math.pi
        rho_next = (jnp.sqrt(1.0 - rho_now * rho_now) + (math.pi - angle_now) * rho_now) / math.pi
        theta = theta * zero_order + rho_next
        rho_now = rho_next
    return theta / (inv_left[:, None] * inv_right[None, :])


def apply_inverse(values, inverse):
    return lax.dot_general(
        values,
        inverse,
        (((1,), (1,)), ((), ())),
        precision=lax.Precision.HIGHEST,
        preferred_element_type=jnp.float32,
    )


def on_device(panel, centres_cols, centres_rows, diag_inverse, trailing):
    col_count = lax.axis_size("col")
    target_rank = col_count // 4
    block_ids = jnp.arange(col_count, dtype=jnp.int32)
    panel_at = jnp.sum(jnp.where(panel == target_rank, block_ids, 0))
    panel_x = broadcast(centres_cols, "col", panel_at)
    panel_inv = broadcast(diag_inverse, "col", panel_at)

    def panel_rows_of(piece):
        return apply_inverse(kernel(piece, panel_x), panel_inv)

    rows_l = panel_rows_of(lax.all_gather(centres_rows, "col", axis=0, tiled=True))
    cols_l = panel_rows_of(centres_cols)
    update = lax.dot_general(
        rows_l,
        cols_l,
        (((1,), (1,)), ((), ())),
        precision=lax.Precision.HIGHEST,
        preferred_element_type=jnp.float32,
    )
    block_here = lax.axis_index("col")
    own_rank = lax.dynamic_index_in_dim(panel, block_here, 0, keepdims=False)
    return jnp.where(own_rank > target_rank, trailing - update, trailing)


def solution(mesh):
    return jax.shard_map(
        on_device,
        mesh=mesh,
        in_specs=(P(), P("col", None), P(("row", "col"), None), P("col", None), P("row", "col")),
        out_specs=P("row", "col"),
        check_vma=False,
    )
```

profile of v0, /device:TPU:1, one launch (start us, length us, event | category | flops | bytes accessed | tf_op | source)
XLA Modules:
  0.0 512.0 jit_solution(12042767771723486847)
XLA Ops:
  6.5 0.0 all-reduce.3.cloned.1.call-start
  6.5 1.3 fusion.110
  8.5 1.1 broadcast_select_fusion
  9.5 0.0 copy-start.2
  9.6 0.0 all-reduce.3.cloned.1.call-update
  9.6 0.0 all-reduce.5.cloned.1.call-start
  9.6 1.1 copy-done.2
  10.8 1.1 broadcast_select_fusion.1
  11.8 0.0 copy-start.5
  11.8 0.0 copy-start
  11.8 0.0 all-reduce.5.cloned.1.call-update
  11.9 0.0 all-gather.3.cloned.1.call-start
  11.9 0.7 all-gather.3.cloned.1.call-update
  12.6 0.0 copy-done.5
  12.6 0.6 dynamic_slice.4
  13.8 0.0 copy-done
  13.9 0.3 multiply_reduce_fusion
  14.1 197.4 %all-reduce.3.cloned.1.call-done = bf16[512,1024]{1,0:T(8,128)(2,1)} async-done(((bf16[512,1024]{1,0:T(8,128)(2,1)}), bf16[512,1024]{1,0:T(8,128)(2,1)}) %all-reduce.3.cloned.1.call-update) | async-done | bytes 1048592 | tf_op jit(solution)/shard_map/psum | solution.py:12
  211.6 0.0 copy-start.3
  211.6 1.6 multiply_reduce_fusion.1
  213.2 0.0 copy-done.3
  213.2 0.7 fusion.1
  213.9 193.9 %all-reduce.5.cloned.1.call-done = f32[512,512]{1,0:T(8,128)} async-done(((f32[512,512]{1,0:T(8,128)}), f32[512,512]{1,0:T(8,128)}) %all-reduce.5.cloned.1.call-update) | async-done | bytes 1048592 | tf_op jit(solution)/shard_map/psum | solution.py:12
  407.8 12.7 %fusion.4 = f32[512,512]{1,0:T(8,128)S(1)} fusion(f32[512,512]{1,0:T(8,128)} %all-reduce.5.cloned.1.call-done, f32[512,512]{0,1:T(8,128)S(1)} %fusion.1, f32[512]{0:T(512)S(1)} %add_rsqrt_fusion, f32[512]{0:T(512)S(1)} %add_rsqrt_fusion.1), kind=kOutput, calls=%fused_computation.10 | convolution fusion | flops 1620574208 | bytes 3149824 | tf_op jit(solution)/shard_map/dot_general | solution.py:36
  420.5 67.7 %all-gather.3.cloned.1.call-done = bf16[128,4,1024]{2,1,0:T(4,128)(2,1)} async-done(((bf16[1,4,1024]{2,1,0:T(4,128)(2,1)}), bf16[128,4,1024]{2,1,0:T(4,128)(2,1)}) %all-gather.3.cloned.1.call-update) | async-done | bytes 1048592 | tf_op jit(solution)/shard_map/all_gather | solution.py:56
  488.2 1.3 reshape.15
  489.6 0.3 multiply_reduce_fusion.2
  489.8 0.0 copy-start.4
  489.9 0.7 fusion.3
  490.6 0.5 copy-done.4
  491.1 0.0 copy-start.1
  491.1 11.5 %fusion.52 = f32[512,512]{1,0:T(8,128)S(1)} fusion(f32[512,512]{1,0:T(8,128)S(1)} %copy-done.4, f32[512,512]{0,1:T(8,128)S(1)} %fusion.3, f32[512]{0:T(512)S(1)} %add_rsqrt_fusion.1, f32[512]{0:T(512)S(1)} %add_rsqrt_fusion.2), kind=kOutput, calls=%fused_computation.58 | convolution fusion | flops 1620574208 | bytes 3149824 | tf_op jit(solution)/shard_map/dot_general | solution.py:36
  502.6 0.0 copy-done.1
  502.6 2.8 subtract_select_fusion
  (3 shorter events, 0.0 us)
Async XLA Ops:
  6.5 205.0 %all-reduce.3.cloned.1.call-start = ((), (), s32[]{:S(2)}) async-start(), calls=%async_computation | async-start | bytes 2097152 | tf_op jit(solution)/shard_map/psum | solution.py:12
  9.5 1.2 copy-start.2
  9.6 398.3 %all-reduce.5.cloned.1.call-start = ((), (), s32[]{:S(2)}) async-start(), calls=%async_computation.1 | async-start | bytes 2097152 | tf_op jit(solution)/shard_map/psum | solution.py:12
  11.8 0.8 copy-start.5
  11.8 2.0 copy-start
  11.9 476.3 %all-gather.3.cloned.1.call-start = ((), (), s32[]{:S(2)}) async-start(), calls=%async_computation.2 | async-start | bytes 1056768 | tf_op jit(solution)/shard_map/all_gather | solution.py:56
  211.6 1.6 copy-start.3
  489.8 1.2 copy-start.4
  491.1 11.5 %copy-start.1 = (f32[512,512]{1,0:T(8,128)S(1)}, f32[512,512]{1,0:T(8,128)}, u32[]{:S(2)}) copy-start(f32[512,512]{1,0:T(8,128)} %param.9) | copy-start | bytes 3145732
Sparse Core Ops, SparseCore 0:
  10.6 200.9 all-reduce.2
  214.8 193.0 all-reduce.4
  410.9 77.2 all-gather.2
where the time goes:
time: 512 us
  waiting for transfers between devices  460 us (90%)
  matrix products  28.5 us (6%)
  between operations  14.5 us (3%)
  other arithmetic  5.59 us (1%)
    psum x2, waiting for transfers between devices, broadcast(): return lax.psum(jnp.where(mine, shard, jnp.zeros_like(shard)), axis)  391 us
    all_gather x1, waiting for transfers between devices, on_device(): lax.all_gather(centres_rows, 'col', axis=0, tiled=True)  67.7 us
    dot_general x2, matrix products, apply_inverse(): lax.dot_general(values, inverse, (((1,), (1,)), ((), ())), precision=lax....  24.2 us
  transfers between devices with their start and end apart: 3, of which 3 were waited for; matrix products, arithmetic and copies ran while one was open for 3% of the time, Pallas kernels for 0%

commit v1 on v0

--- a/solution.py
+++ b/solution.py
@@ -53,7 +53,11 @@
     def panel_rows_of(piece):
         return apply_inverse(kernel(piece, panel_x), panel_inv)
 
-    rows_l = panel_rows_of(lax.all_gather(centres_rows, "col", axis=0, tiled=True))
+    rows_l = panel_rows_of(
+        jnp.concatenate(
+            lax.all_to_all(jnp.stack([centres_rows] * lax.axis_size("col")), "col", 0, 0), axis=0
+        )
+    )
     cols_l = panel_rows_of(centres_cols)
     update = lax.dot_general(
         rows_l,

time: 512 us -> 464 us (0.906)
  waiting for transfers between devices: 460 us -> 388 us
  starting transfers between devices: 0.09 us -> 18.8 us
    all_gather x1 -> x0, waiting for transfers between devices: 67.7 us -> none  [on_device(): lax.all_gather(centres_rows, 'col', axis=0, tiled=True)]
    all_to_all x0 -> x1, starting transfers between devices: none -> 18.6 us  [on_device(): lax.all_to_all(jnp.stack([centres_rows] * lax.axis_size('col')), 'col', 0...]
  transfers between devices with their start and end apart: 3 -> 3, of which waited for: 3 -> 2; matrix products, arithmetic and copies ran while one was open for 3% -> 4% of each run, Pallas kernels for 0% -> 0%
where the time goes in v1:
time: 464 us; the launch traced here: 463 us
  waiting for transfers between devices  388 us (84%)
  matrix products  30.9 us (7%)
  starting transfers between devices  18.8 us (4%)
  between operations  14.8 us (3%)
  other arithmetic  5.69 us (1%)
    psum x2, waiting for transfers between devices, broadcast(): return lax.psum(jnp.where(mine, shard, jnp.zeros_like(shard)), axis)  388 us
    dot_general x2, matrix products, apply_inverse(): lax.dot_general(values, inverse, (((1,), (1,)), ((), ())), precision=lax....  24.3 us
    all_to_all x1, starting transfers between devices, on_device(): lax.all_to_all(jnp.stack([centres_rows] * lax.axis_size('col')), 'col', 0...  18.6 us
  transfers between devices with their start and end apart: 3, of which 2 were waited for; matrix products, arithmetic and copies ran while one was open for 4% of the time, Pallas kernels for 0%

profile of v1, /device:TPU:1, one launch (start us, length us, event | category | flops | bytes accessed | tf_op | source)
XLA Modules:
  0.0 462.9 jit_solution(11941349508006157494)
XLA Ops:
  6.5 0.0 all-reduce.3.cloned.1.call-start
  6.5 1.3 fusion.110
  8.5 1.1 broadcast_select_fusion
  9.5 0.0 copy-start.4
  9.5 0.0 all-reduce.3.cloned.1.call-update
  9.6 0.7 copy-done.4
  10.2 1.3 stack.2
  11.5 0.0 copy-start.2
  11.6 18.6 %all-to-all-start = ((bf16[128,4,1024]{2,1,0:T(4,128)(2,1)}), bf16[128,4,1024]{2,1,0:T(4,128)(2,1)S(1)}, u32[]{:S(2)}, u32[]{:S(2)}) async-start(bf16[128,4,1024]{2,1,0:T(4,128)(2,1)} %stack.2), calls=%async_computation | async-start | bytes 2097152 | tf_op jit(solution)/shard_map/all_to_all | solution.py:58
  30.1 0.2 all-reduce.5.cloned.1.call-start
  30.3 0.0 copy-done.2
  30.4 1.1 broadcast_select_fusion.1
  31.4 0.0 copy-start.6
  31.4 0.0 copy-start
  31.4 0.0 all-reduce.5.cloned.1.call-update
  31.4 0.6 copy-done.6
  32.1 0.6 dynamic_slice.4
  33.3 0.0 copy-done
  33.3 0.3 multiply_reduce_fusion
  33.6 195.2 %all-reduce.3.cloned.1.call-done = bf16[512,1024]{1,0:T(8,128)(2,1)} async-done(((bf16[512,1024]{1,0:T(8,128)(2,1)}), bf16[512,1024]{1,0:T(8,128)(2,1)}) %all-reduce.3.cloned.1.call-update) | async-done | bytes 1048592 | tf_op jit(solution)/shard_map/psum | solution.py:12
  228.8 0.0 copy-start.3
  228.8 1.6 multiply_reduce_fusion.1
  230.4 0.0 copy-done.3
  230.4 1.7 fusion.1
  232.1 192.9 %all-reduce.5.cloned.1.call-done = f32[512,512]{1,0:T(8,128)} async-done(((f32[512,512]{1,0:T(8,128)}), f32[512,512]{1,0:T(8,128)}) %all-reduce.5.cloned.1.call-update) | async-done | bytes 1048592 | tf_op jit(solution)/shard_map/psum | solution.py:12
  425.1 13.0 %fusion.4 = f32[512,512]{1,0:T(8,128)S(1)} fusion(f32[512,512]{1,0:T(8,128)} %all-reduce.5.cloned.1.call-done, f32[512,512]{0,1:T(8,128)} %fusion.1, f32[512]{0:T(512)S(1)} %add_rsqrt_fusion, f32[512]{0:T(512)S(1)} %add_rsqrt_fusion.1), kind=kOutput, calls=%fused_computation.10 | convolution fusion | flops 1620574208 | bytes 3149824 | tf_op jit(solution)/shard_map/dot_general | solution.py:36
  438.1 0.0 all-to-all-done
  438.1 0.4 multiply_reduce_fusion.2
  438.5 0.1 copy.12
  438.6 0.1 sqrt.31
  438.7 1.1 reshape.26
  439.8 0.0 copy-start.5
  439.9 2.1 fusion.3
  441.9 0.0 copy-done.5
  441.9 0.0 copy-start.1
  441.9 11.3 %fusion.52 = f32[512,512]{1,0:T(8,128)S(1)} fusion(f32[512,512]{1,0:T(8,128)S(1)} %copy-done.5, f32[512,512]{0,1:T(8,128)S(1)} %fusion.3, f32[512]{0:T(512)S(1)} %add_rsqrt_fusion.1, f32[512]{0:T(512)S(1)} %sqrt.31), kind=kOutput, calls=%fused_computation.58 | convolution fusion | flops 1620574208 | bytes 3149824 | tf_op jit(solution)/shard_map/dot_general | solution.py:36
  453.2 0.0 copy-done.1
  453.2 2.8 subtract_select_fusion
  (3 shorter events, 0.0 us)
Async XLA Ops:
  6.5 222.2 %all-reduce.3.cloned.1.call-start = ((), (), s32[]{:S(2)}) async-start(), calls=%async_computation.1 | async-start | bytes 2097152 | tf_op jit(solution)/shard_map/psum | solution.py:12
  9.5 0.7 copy-start.4
  11.5 18.8 %copy-start.2 = (f32[512,512]{1,0:T(8,128)S(1)}, f32[512,512]{1,0:T(8,128)}, u32[]{:S(2)}) copy-start(f32[512,512]{1,0:T(8,128)} %param.8) | copy-start | bytes 3145732
  11.6 426.6 %all-to-all-start = ((bf16[128,4,1024]{2,1,0:T(4,128)(2,1)}), bf16[128,4,1024]{2,1,0:T(4,128)(2,1)S(1)}, u32[]{:S(2)}, u32[]{:S(2)}) async-start(bf16[128,4,1024]{2,1,0:T(4,128)(2,1)} %stack.2), calls=%async_computation | async-start | bytes 2097152 | tf_op jit(solution)/shard_map/all_to_all | solution.py:58
  30.1 395.0 %all-reduce.5.cloned.1.call-start = ((), (), s32[]{:S(2)}) async-start(), calls=%async_computation.2 | async-start | bytes 2097152 | tf_op jit(solution)/shard_map/psum | solution.py:12
  31.4 0.7 copy-start.6
  31.4 1.9 copy-start
  228.8 1.6 copy-start.3
  439.8 2.1 copy-start.5
  441.9 11.3 %copy-start.1 = (f32[512,512]{1,0:T(8,128)S(1)}, f32[512,512]{1,0:T(8,128)}, u32[]{:S(2)}) copy-start(f32[512,512]{1,0:T(8,128)} %param.9) | copy-start | bytes 3145732
Sparse Core Ops, SparseCore 0:
  10.6 218.1 all-reduce.2
  232.0 193.0 all-reduce.4
